TPU v7x, 32 devices: a whole 2x2x4 slice. The times are simulated.
32 devices in a mesh: groups: 2 (over y), expert: 8 (over z, x), dp: 2 (over core).
Axes of the slice: x: 2, y: 2, z: 4, core: 2. Of those that a mesh axis runs over, the one named last changes fastest.
Arguments:
- tokens: bfloat16 [4096, 3584], P(('groups', 'expert', 'dp')), parts along dimension 0, may hold values from -6 to 6
- grad_out: bfloat16 [4096, 3584], P(('groups', 'expert', 'dp')), parts along dimension 0, may hold values from -6 to 6
- routing: int32 [4096, 8], P(('groups', 'expert', 'dp')), parts along dimension 0, may hold values from 0 to 63, as said below
- gates: float32 [4096, 8], P(('groups', 'expert', 'dp')), parts along dimension 0, may hold values from 0.05 to 0.5
- modality: int32 [4096], P(('groups', 'expert', 'dp')), parts along dimension 0, may hold values from 0 to 1, as said below
- hot_experts: int32 [4], P('groups'), parts along dimension 0, may hold values from 0 to 7, as said below
- gate_weight: bfloat16 [16384, 3584], P('expert'), may hold values from -0.09375 to 0.09375
- up_weight: bfloat16 [16384, 3584], P('expert'), may hold values from -0.09375 to 0.09375
- down_weight: bfloat16 [16384, 3584], P('expert'), may hold values from -0.125 to 0.125
Outputs:
- grad_tokens: bfloat16 [4096, 3584], P(('groups', 'expert', 'dp')), parts along dimension 0
- grad_gate: bfloat16 [32768, 3584], P(('groups', 'expert', 'dp')), parts along dimension 0
- grad_up: bfloat16 [32768, 3584], P(('groups', 'expert', 'dp')), parts along dimension 0
- grad_down: bfloat16 [32768, 3584], P(('groups', 'expert', 'dp')), parts along dimension 0
There are 2 independent parts, one for each index of `groups`. A program takes and returns all parts, laid end to end along the dimension named above; an argument that names none is the same for every part. Nothing has to cross between parts.
Inputs may be any that keep to these rules, and one draw needn't show every extreme that they name: `routing`: each token names 8 different experts. Among the 128 tokens of each device, every expert in flight that is not hot is named by exactly 2 text tokens, a text token names at most one expert in flight, an image token names none in flight outside its last 2 entries, and no text token names a hot expert. `modality`: exactly 8 image tokens among the 128 tokens of each device. `hot_experts`: 2 different experts in flight.
All inputs are finite; a program needn't handle non-finite values.
Results may differ from a plain program's by a relative error of at most 0.0061.
Values may be sent and summed in bfloat16 or wider, within the bound.
No kernel may reach another device: no remote copies, remote signals or barrier semaphores. Data moves between devices by JAX's collectives and lax.ppermute only.
A program may use at most 384 MiB of HBM per device.

v0:
```python
import jax
import jax.numpy as jnp
from jax import lax
from jax.sharding import PartitionSpec as P

FLIGHT = 8
HOTCAP = 8


def expert_pass(in_tokens, in_scaled, gate_rows, up_rows, down_rows):
    pre_gate = jnp.einsum("nd,hd->nh", in_tokens, gate_rows, preferred_element_type=jnp.float32)
    pre_up = jnp.einsum("nd,hd->nh", in_tokens, up_rows, preferred_element_type=jnp.float32)
    sigmoid_gate = jax.nn.sigmoid(pre_gate)
    swish_gate = pre_gate * sigmoid_gate
    activated = (swish_gate * pre_up).astype(jnp.bfloat16)
    grad_act = jnp.einsum("nd,hd->nh", in_scaled, down_rows, preferred_element_type=jnp.float32)
    grad_pre_gate = (
        grad_act * pre_up * sigmoid_gate * (1.0 + pre_gate * (1.0 - sigmoid_gate))
    ).astype(jnp.bfloat16)
    grad_pre_up = (grad_act * swish_gate).astype(jnp.bfloat16)
    gate_term = jnp.einsum(
        "nh,nd->hd", grad_pre_gate, in_tokens, preferred_element_type=jnp.float32
    )
    up_term = jnp.einsum("nh,nd->hd", grad_pre_up, in_tokens, preferred_element_type=jnp.float32)
    down_term = jnp.einsum("nh,nd->hd", activated, in_scaled, preferred_element_type=jnp.float32)
    partials = jnp.dot(grad_pre_gate, gate_rows, preferred_element_type=jnp.float32)
    partials = (
        partials + jnp.dot(grad_pre_up, up_rows, preferred_element_type=jnp.float32)
    ).astype(jnp.bfloat16)
    return (partials, (gate_term, up_term, down_term))


def per_device(
    tokens, grad_out, routing, gates, modality, hot_experts, gate_weight, up_weight, down_weight
):
    tok_count, model_width = tokens.shape
    top_count = routing.shape[1]
    hot_count = hot_experts.shape[0]
    devices = lax.axis_size("expert")
    split_count = devices // FLIGHT
    position = lax.broadcasted_iota(jnp.int32, (tok_count, top_count), 1)
    pinned_slot = position - (top_count - hot_count)
    pick_table = pinned_slot[:, :, None] == jnp.arange(hot_count, dtype=jnp.int32)[None, None, :]
    hot_pick = jnp.sum(jnp.where(pick_table, hot_experts[None, None, :], 0), axis=2)
    pinned = (modality[:, None] == 1) & (pinned_slot >= 0)
    chosen = jnp.where(pinned, hot_pick, routing)
    matches = chosen[:, :, None] == jnp.arange(FLIGHT, dtype=jnp.int32)[None, None, :]
    expert_gate = jnp.sum(jnp.where(matches, gates[:, :, None], 0.0), axis=1)
    present = jnp.any(matches, axis=1)
    placed = jnp.cumsum(present.astype(jnp.int32), axis=0) - 1
    slot_ids = jnp.arange(HOTCAP, dtype=jnp.int32)
    chooser = (placed.T[:, None, :] == slot_ids[None, :, None]) & present.T[:, None, :]
    picker = chooser.astype(jnp.bfloat16)
    picked = jnp.einsum("scr,rd->scd", picker, tokens, preferred_element_type=jnp.float32).astype(
        jnp.bfloat16
    )
    picked_grad = jnp.einsum("scr,rd->scd", picker, grad_out, preferred_element_type=jnp.float32)
    slot_gate = jnp.sum(jnp.where(chooser, expert_gate.T[:, None, :], 0.0), axis=2)
    scaled = (picked_grad * slot_gate[:, :, None]).astype(jnp.bfloat16)
    picked, scaled = (picked, scaled)
    send_shape = (devices, HOTCAP, model_width)

    def replicate_rows(block_data):
        widened = jnp.broadcast_to(block_data[:, None], (FLIGHT, split_count, HOTCAP, model_width))
        return widened.reshape(send_shape)

    got_tokens, got_scaled = (
        lax.all_to_all(replicate_rows(picked), "expert", split_axis=0, concat_axis=0, tiled=True),
        lax.all_to_all(replicate_rows(scaled), "expert", split_axis=0, concat_axis=0, tiled=True),
    )
    partials, grad_terms = expert_pass(
        got_tokens.reshape(-1, model_width),
        got_scaled.reshape(-1, model_width),
        gate_weight,
        up_weight,
        down_weight,
    )
    returned = lax.all_to_all(
        partials.reshape(send_shape), "expert", split_axis=0, concat_axis=0, tiled=True
    )
    returned = returned.reshape(FLIGHT, split_count, HOTCAP, model_width)
    grad_tokens = jnp.einsum(
        "fcr,fpcd->rd", chooser.astype(jnp.bfloat16), returned, preferred_element_type=jnp.float32
    )
    summed = (
        lax.psum_scatter(grad_terms[0], "dp", scatter_dimension=0, tiled=True),
        lax.psum_scatter(grad_terms[1], "dp", scatter_dimension=0, tiled=True),
        lax.psum_scatter(grad_terms[2], "dp", scatter_dimension=0, tiled=True),
    )
    return (
        grad_tokens.astype(jnp.bfloat16),
        summed[0].astype(jnp.bfloat16),
        summed[1].astype(jnp.bfloat16),
        summed[2].astype(jnp.bfloat16),
    )


def solution(mesh):
    in_specs = (
        P(("groups", "expert", "dp"), None),
        P(("groups", "expert", "dp"), None),
        P(("groups", "expert", "dp"), None),
        P(("groups", "expert", "dp"), None),
        P(("groups", "expert", "dp")),
        P("groups"),
        P("expert", None),
        P("expert", None),
        P("expert", None),
    )
    out_specs = (
        P(("groups", "expert", "dp"), None),
        P(("groups", "expert", "dp"), None),
        P(("groups", "expert", "dp"), None),
        P(("groups", "expert", "dp"), None),
    )
    return jax.shard_map(
        per_device, mesh=mesh, in_specs=in_specs, out_specs=out_specs, check_vma=False
    )
```

profile of v0, /device:TPU:0, one launch (start us, length us, event | category | flops | bytes accessed | tf_op | source)
XLA Modules:
  0.0 211.0 jit_solution(14166473032863376491)
XLA Ops:
  7.2 0.7 broadcast_compare_fusion.1
  7.9 0.7 select_reduce_fusion.2
  8.7 0.8 and_select_fusion
  9.5 0.1 copy.28
  9.6 0.2 reduce_window_sum.11
  9.8 1.0 convolution_convert_fusion
  10.9 7.3 %all-to-all-start.1 = ((bf16[8,8,3584]{2,1,0:T(8,128)(2,1)}), bf16[8,8,3584]{2,1,0:T(8,128)(2,1)S(1)}, u32[]{:S(2)}, u32[]{:S(2)}) async-start(bf16[8,8,3584]{2,1,0:T(8,128)(2,1)} %convolution_convert_fusion), calls=%async_computation.1 | async-start | bytes 917504 | tf_op jit(solution)/shard_map/all_to_all | solution.py:68
  18.1 0.7 select_reduce_fusion.1
  18.8 0.1 select_reduce_fusion
  18.9 0.1 copy.31
  19.0 2.2 %fusion.1 = bf16[8,8,3584]{2,1,0:T(8,128)(2,1)} fusion(bf16[128,3584]{1,0:T(8,128)(2,1)} %param.10, f32[8,8]{1,0:T(8,128)S(1)} %copy.31, pred[8,8,128]{2,0,1:T(8,128)(4,1)S(1)} %fusion.22), kind=kOutput, calls=%fused_computation.5 | convolution fusion | flops 59179008 | bytes 1384704 | tf_op jit(solution)/shard_map/scr,rd->scd/dot_general | solution.py:57
  21.2 10.0 %all-to-all-done.1 = bf16[8,8,3584]{2,1,0:T(8,128)(2,1)S(1)} async-done(((bf16[8,8,3584]{2,1,0:T(8,128)(2,1)}), bf16[8,8,3584]{2,1,0:T(8,128)(2,1)S(1)}, u32[]{:S(2)}, u32[]{:S(2)}) %all-to-all-start.1) | async-done | bytes 458784 | tf_op jit(solution)/shard_map/all_to_all | solution.py:68
  31.2 3.6 %all-to-all-start = ((bf16[8,8,3584]{2,1,0:T(8,128)(2,1)}), bf16[8,8,3584]{2,1,0:T(8,128)(2,1)S(1)}, u32[]{:S(2)}, u32[]{:S(2)}) async-start(bf16[8,8,3584]{2,1,0:T(8,128)(2,1)} %fusion.1), calls=%async_computation | async-start | bytes 917504 | tf_op jit(solution)/shard_map/all_to_all | solution.py:69
  34.9 0.0 reduce-scatter.8.cloned.1.call-start
  34.9 9.7 %fusion.11 = f32[64,2048]{1,0:T(8,128)S(1)} fusion(bf16[2048,3584]{1,0:T(8,128)(2,1)} %param.15, bf16[8,8,3584]{2,1,0:T(8,128)(2,1)S(1)} %all-to-all-done.1), kind=kOutput, calls=%fused_computation.19 | convolution fusion | flops 939524096 | bytes 15663104 | tf_op jit(solution)/shard_map/nd,hd->nh/dot_general | solution.py:11
  44.6 9.7 %fusion.13 = f32[64,2048]{1,0:T(8,128)S(1)} fusion(bf16[2048,3584]{1,0:T(8,128)(2,1)} %param.16, bf16[8,8,3584]{2,1,0:T(8,128)(2,1)S(1)} %all-to-all-done.1), kind=kOutput, calls=%fused_computation.21 | convolution fusion | flops 939524096 | bytes 15663104 | tf_op jit(solution)/shard_map/nd,hd->nh/dot_general | solution.py:12
  54.2 11.7 %fusion.15 = f32[2048,3584]{1,0:T(8,128)} fusion(bf16[8,8,3584]{2,1,0:T(8,128)(2,1)S(1)} %all-to-all-done, f32[64,2048]{1,0:T(8,128)S(1)} %fusion.13, f32[64,2048]{1,0:T(8,128)S(1)} %fusion.11), kind=kOutput, calls=%fused_computation.23 | convolution fusion | flops 940310528 | bytes 30867456 | tf_op jit(solution)/shard_map/nh,nd->hd/dot_general | solution.py:25
  65.9 0.0 reduce-scatter.8.cloned.1.call-update
  66.0 0.0 reduce-scatter.6.cloned.1.call-start
  66.0 9.7 %multiply_convert_fusion.1 = (bf16[64,2048]{1,0:T(8,128)(2,1)S(1)}, bf16[64,2048]{1,0:T(8,128)(2,1)S(1)}) fusion(f32[64,2048]{1,0:T(8,128)S(1)} %fusion.11, f32[64,2048]{1,0:T(8,128)S(1)} %fusion.13, bf16[2048,3584]{1,0:T(8,128)(2,1)} %param.17, bf16[8,8,3584]{2,1,0:T(8,128)(2,1)S(1)} %all-to-all-done), kind=kOutput, calls=%fused_computation.11 | convolution fusion | flops 941228032 | bytes 16711680 | tf_op jit(solution)/shard_map/nd,hd->nh/dot_general | solution.py:16
  75.7 19.1 %fusion.7 = f32[2048,3584]{1,0:T(8,128)} fusion(bf16[64,2048]{1,0:T(8,128)(2,1)S(1)} %get-tuple-element.4, bf16[8,8,3584]{2,1,0:T(8,128)(2,1)S(1)} %all-to-all-done.1), kind=kOutput, calls=%fused_computation.15 | convolution fusion | flops 939524096 | bytes 30081024 | tf_op jit(solution)/shard_map/nh,nd->hd/dot_general | solution.py:24
  94.8 0.0 reduce-scatter.6.cloned.1.call-update
  94.9 0.2 reduce-scatter.4.cloned.1.call-start
  95.1 15.1 %fusion.9 = f32[2048,3584]{1,0:T(8,128)} fusion(bf16[64,2048]{1,0:T(8,128)(2,1)S(1)} %get-tuple-element.5, bf16[8,8,3584]{2,1,0:T(8,128)(2,1)S(1)} %all-to-all-done.1), kind=kOutput, calls=%fused_computation.17 | convolution fusion | flops 939524096 | bytes 30081024 | tf_op jit(solution)/shard_map/nh,nd->hd/dot_general | solution.py:21
  110.2 7.8 %fusion.27 = f32[64,3584]{1,0:T(8,128)S(1)} fusion(bf16[64,2048]{1,0:T(8,128)(2,1)S(1)} %get-tuple-element.5, bf16[2048,3584]{1,0:T(8,128)(2,1)} %param.15), kind=kOutput, calls=%fused_computation.44 | convolution fusion | flops 939524096 | bytes 15859712 | tf_op jit(solution)/shard_map/dot_general | solution.py:26
  118.0 10.4 %fusion.3 = bf16[8,8,3584]{2,1,0:T(8,128)(2,1)S(1)} fusion(f32[64,3584]{1,0:T(8,128)S(1)} %fusion.27, bf16[64,2048]{1,0:T(8,128)(2,1)S(1)} %get-tuple-element.4, bf16[2048,3584]{1,0:T(8,128)(2,1)} %param.16), kind=kOutput, calls=%fused_computation.7 | convolution fusion | flops 939982848 | bytes 16318464 | tf_op jit(solution)/shard_map/dot_general | solution.py:28
  128.4 18.5 %all_to_all.15 = bf16[8,8,3584]{2,1,0:T(8,128)(2,1)S(1)} all-to-all(bf16[8,8,3584]{2,1,0:T(8,128)(2,1)S(1)} %fusion.3), channel_id=1, replica_groups=mesh['groups'=2,'expert'=8,'dp'=2] {'expert'}, dimensions={0} | all-to-all | bytes 917504 | tf_op jit(solution)/shard_map/all_to_all | solution.py:78
  146.9 1.4 fusion
  148.3 9.6 %convert_element_type.46 = bf16[1024,3584]{1,0:T(8,128)(2,1)} convert(f32[1024,3584]{1,0:T(8,128)} %reduce-scatter.8.cloned.1.call-done) | non-fusion elementwise | flops 3670016 | bytes 22020096 | tf_op jit(solution)/shard_map/convert_element_type | solution.py:94
  157.9 12.1 %convert_element_type.44 = bf16[1024,3584]{1,0:T(8,128)(2,1)} convert(f32[1024,3584]{1,0:T(8,128)} %reduce-scatter.6.cloned.1.call-done) | non-fusion elementwise | flops 3670016 | bytes 22020096 | tf_op jit(solution)/shard_map/convert_element_type | solution.py:93
  170.0 25.3 %reduce-scatter.4.cloned.1.call-done = f32[1024,3584]{1,0:T(8,128)} async-done(((f32[2048,3584]{1,0:T(8,128)}), f32[1024,3584]{1,0:T(8,128)}) %reduce-scatter.4.cloned.1.call-update) | async-done | bytes 14680080 | tf_op jit(solution)/shard_map/reduce_scatter | solution.py:86
  195.4 9.1 %convert_element_type.43 = bf16[1024,3584]{1,0:T(8,128)(2,1)} convert(f32[1024,3584]{1,0:T(8,128)} %reduce-scatter.4.cloned.1.call-done) | non-fusion elementwise | flops 3670016 | bytes 22020096 | tf_op jit(solution)/shard_map/convert_element_type | solution.py:92
  (15 shorter events, 0.2 us)
Async XLA Ops:
  7.2 2.7 %copy-start = (bf16[128,3584]{1,0:T(8,128)(2,1)S(1)}, bf16[128,3584]{1,0:T(8,128)(2,1)}, u32[]{:S(2)}) copy-start(bf16[128,3584]{1,0:T(8,128)(2,1)} %param.9) | copy-start | bytes 2752516
  10.9 20.3 %all-to-all-start.1 = ((bf16[8,8,3584]{2,1,0:T(8,128)(2,1)}), bf16[8,8,3584]{2,1,0:T(8,128)(2,1)S(1)}, u32[]{:S(2)}, u32[]{:S(2)}) async-start(bf16[8,8,3584]{2,1,0:T(8,128)(2,1)} %convolution_convert_fusion), calls=%async_computation.1 | async-start | bytes 917504 | tf_op jit(solution)/shard_map/all_to_all | solution.py:68
  31.2 23.0 %all-to-all-start = ((bf16[8,8,3584]{2,1,0:T(8,128)(2,1)}), bf16[8,8,3584]{2,1,0:T(8,128)(2,1)S(1)}, u32[]{:S(2)}, u32[]{:S(2)}) async-start(bf16[8,8,3584]{2,1,0:T(8,128)(2,1)} %fusion.1), calls=%async_computation | async-start | bytes 917504 | tf_op jit(solution)/shard_map/all_to_all | solution.py:69
  34.9 113.4 %reduce-scatter.8.cloned.1.call-start = ((), (), s32[]{:S(2)}) async-start(), calls=%async_computation.8 | async-start | bytes 44040192 | tf_op jit(solution)/shard_map/reduce_scatter | solution.py:88
  66.0 91.9 %reduce-scatter.6.cloned.1.call-start = ((), (), s32[]{:S(2)}) async-start(), calls=%async_computation.7 | async-start | bytes 44040192 | tf_op jit(solution)/shard_map/reduce_scatter | solution.py:87
  94.9 100.5 %reduce-scatter.4.cloned.1.call-start = ((), (), s32[]{:S(2)}) async-start(), calls=%async_computation.6 | async-start | bytes 44040192 | tf_op jit(solution)/shard_map/reduce_scatter | solution.py:86
  157.9 46.6 %copy-start.1 = (bf16[128,3584]{1,0:T(8,128)(2,1)S(1)}, bf16[128,3584]{1,0:T(8,128)(2,1)}, u32[]{:S(2)}) copy-start(bf16[128,3584]{1,0:T(8,128)(2,1)} %param.9) | copy-start | bytes 2752516
Sparse Core Ops, SparseCore 0:
  66.1 41.7 reduce-scatter.7
  110.1 41.4 reduce-scatter.5
  153.9 41.3 reduce-scatter.3
where the time goes:
time: 212 us; the launch traced here: 211 us
  matrix products  97.8 us (46%)
  waiting for transfers between devices  35.4 us (17%)
  other arithmetic  34.1 us (16%)
  blocking collectives  18.5 us (9%)
  between operations  13.8 us (7%)
  starting transfers between devices  11.2 us (5%)
    reduce_scatter x1, waiting for transfers between devices, per_device(): lax.psum_scatter(grad_terms[0], 'dp', scatter_dimension=0, tiled=True)  25.3 us
    dot_general x1, matrix products, expert_pass(): jnp.einsum('nh,nd->hd', grad_pre_up, in_tokens, preferred_element_type=jn...  19.1 us
    all_to_all x1, blocking collectives, per_device(): lax.all_to_all(partials.reshape(send_shape), 'expert', split_axis=0, conc...  18.5 us
    dot_general x1, matrix products, expert_pass(): jnp.einsum('nh,nd->hd', grad_pre_gate, in_tokens, preferred_element_type=...  15.1 us
    convert_element_type x1, other arithmetic, per_device(): summed[1].astype(jnp.bfloat16)  12.1 us
    dot_general x1, matrix products, expert_pass(): jnp.einsum('nh,nd->hd', activated, in_scaled, preferred_element_type=jnp....  11.7 us
    dot_general x1, matrix products, expert_pass(): jnp.dot(grad_pre_up, up_rows, preferred_element_type=jnp.float32)  10.4 us
    all_to_all x1, waiting for transfers between devices, per_device(): lax.all_to_all(replicate_rows(picked), 'expert', split_axis=0, concat_axi...  10 us
  transfers between devices with their start and end apart: 5, of which 2 were waited for; matrix products, arithmetic and copies ran while one was open for 51% of the time, Pallas kernels for 0%

commit v1 on v0

--- a/solution.py
+++ b/solution.py
@@ -5,6 +5,23 @@
 
 FLIGHT = 8
 HOTCAP = 8
+
+
+def wrap_the_area(work_x):
+    ax_name = "expert"
+    b_next, e_now = (lax.axis_size(ax_name), lax.axis_index(ax_name))
+    v_next = list(work_x.shape)
+    arr_now = work_x.shape[0] // b_next
+    v_next[0] = arr_now
+    w1 = v_next[0]
+    v_next[0] = w1 * b_next
+    r_now = jnp.zeros(v_next, work_x.dtype)
+    for m in range(b_next):
+        block_now = lax.dynamic_slice_in_dim(work_x, (e_now ^ m) * arr_now, arr_now, axis=0)
+        if m:
+            block_now = lax.ppermute(block_now, ax_name, [(t, t ^ m) for t in range(b_next)])
+        r_now = lax.dynamic_update_slice_in_dim(r_now, block_now, (e_now ^ m) * w1, axis=0)
+    return r_now
 
 
 def expert_pass(in_tokens, in_scaled, gate_rows, up_rows, down_rows):
@@ -65,7 +82,7 @@
         return widened.reshape(send_shape)
 
     got_tokens, got_scaled = (
-        lax.all_to_all(replicate_rows(picked), "expert", split_axis=0, concat_axis=0, tiled=True),
+        wrap_the_area(replicate_rows(picked)),
         lax.all_to_all(replicate_rows(scaled), "expert", split_axis=0, concat_axis=0, tiled=True),
     )
     partials, grad_terms = expert_pass(

time: 212 us -> 227 us (1.071)
  waiting for transfers between devices: 35.4 us -> 44 us
  starting transfers between devices: 11.2 us -> 19.4 us
    ppermute x0 -> x7, starting transfers between devices: none -> 14.2 us  [wrap_the_area(): lax.ppermute(block_now, ax_name, [(t, t ^ m) for t in range(b_next)])]
    all_to_all x1 -> x0, waiting for transfers between devices: 10 us -> none  [per_device(): lax.all_to_all(replicate_rows(picked), 'expert', split_axis=0, concat_axi...]
    reduce_scatter x1, waiting for transfers between devices: 25.3 us -> 34.6 us  [per_device(): lax.psum_scatter(grad_terms[0], 'dp', scatter_dimension=0, tiled=True)]
    ppermute x0 -> x7, waiting for transfers between devices: none -> 8.07 us  [wrap_the_area(): lax.ppermute(block_now, ax_name, [(t, t ^ m) for t in range(b_next)])]
    dot_general x1, matrix products: 19.1 us -> 11.8 us  [expert_pass(): jnp.einsum('nh,nd->hd', grad_pre_up, in_tokens, preferred_element_type=jn...]
    all_to_all x1 -> x0, starting transfers between devices: 7.25 us -> none  [per_device(): lax.all_to_all(replicate_rows(picked), 'expert', split_axis=0, concat_axi...]
    dot_general x1, matrix products: 11.7 us -> 15.6 us  [expert_pass(): jnp.einsum('nh,nd->hd', activated, in_scaled, preferred_element_type=jnp....]
    dot_general x1, matrix products: 15.1 us -> 18.9 us  [expert_pass(): jnp.einsum('nh,nd->hd', grad_pre_gate, in_tokens, preferred_element_type=...]
  transfers between devices with their start and end apart: 5 -> 11, of which waited for: 2 -> 4; matrix products, arithmetic and copies ran while one was open for 51% -> 43% of each run, Pallas kernels for 0% -> 0%
where the time goes in v1:
time: 227 us; the launch traced here: 226 us
  matrix products  96.7 us (43%)
  waiting for transfers between devices  44 us (19%)
  other arithmetic  34.1 us (15%)
  starting transfers between devices  19.4 us (9%)
  blocking collectives  17.9 us (8%)
  between operations  13.9 us (6%)
    reduce_scatter x1, waiting for transfers between devices, per_device(): lax.psum_scatter(grad_terms[0], 'dp', scatter_dimension=0, tiled=True)  34.6 us
    dot_general x1, matrix products, expert_pass(): jnp.einsum('nh,nd->hd', grad_pre_gate, in_tokens, preferred_element_type=...  18.9 us
    all_to_all x1, blocking collectives, per_device(): lax.all_to_all(partials.reshape(send_shape), 'expert', split_axis=0, conc...  17.9 us
    dot_general x1, matrix products, expert_pass(): jnp.einsum('nh,nd->hd', activated, in_scaled, preferred_element_type=jnp....  15.6 us
    ppermute x7, starting transfers between devices, wrap_the_area(): lax.ppermute(block_now, ax_name, [(t, t ^ m) for t in range(b_next)])  14.2 us
    convert_element_type x1, other arithmetic, per_device(): summed[1].astype(jnp.bfloat16)  12.6 us
    dot_general x1, matrix products, expert_pass(): jnp.einsum('nh,nd->hd', grad_pre_up, in_tokens, preferred_element_type=jn...  11.8 us
    dot_general x1, matrix products, expert_pass(): jnp.einsum('nd,hd->nh', in_scaled, down_rows, preferred_element_type=jnp....  9.71 us
  transfers between devices with their start and end apart: 11, of which 4 were waited for; matrix products, arithmetic and copies ran while one was open for 43% of the time, Pallas kernels for 0%

profile of v1, /device:TPU:0, one launch (start us, length us, event | category | flops | bytes accessed | tf_op | source)
XLA Modules:
  0.0 226.4 jit_solution(6558546683668866942)
XLA Ops:
  7.2 0.7 broadcast_compare_fusion.1
  8.0 0.7 select_reduce_fusion.2
  8.7 0.8 and_select_fusion
  9.6 0.2 reduce_window_sum.11
  9.9 0.3 convolution_convert_fusion
  10.2 3.0 %collective-permute-start = (bf16[1,8,3584]{2,1,0:T(8,128)(2,1)S(1)}, bf16[1,8,3584]{2,1,0:T(8,128)(2,1)S(1)}, u32[]{:S(2)}, u32[]{:S(2)}) collective-permute-start(bf16[1,8,3584]{2,1,0:T(8,128)(2,1)S(1)} %get-tuple-element.12), channel_id=1, source_target_pairs={{0,2},{2,0},{4,6},{6,4},{8,10},{10,8},{12,14},{14,12},{1,3},{3,1},... | collective-permute-start | bytes 172040 | tf_op jit(solution)/shard_map/ppermute | solution.py:22
  13.2 1.6 collective-permute-start.1
  14.8 3.0 %collective-permute-start.3 = (bf16[1,8,3584]{2,1,0:T(8,128)(2,1)S(1)}, bf16[1,8,3584]{2,1,0:T(8,128)(2,1)S(1)}, u32[]{:S(2)}, u32[]{:S(2)}) collective-permute-start(bf16[1,8,3584]{2,1,0:T(8,128)(2,1)S(1)} %get-tuple-element.9), channel_id=1, source_target_pairs={{0,8},{2,10},{4,12},{6,14},{8,0},{10,2},{12,4},{14,6},{1,9},{3,11}... | collective-permute-start | bytes 172040 | tf_op jit(solution)/shard_map/ppermute | solution.py:22
  17.8 1.3 collective-permute-start.4
  19.1 0.7 select_reduce_fusion.1
  20.0 2.2 fusion.1
  22.2 4.9 %all-to-all-start = ((bf16[8,8,3584]{2,1,0:T(8,128)(2,1)}), bf16[8,8,3584]{2,1,0:T(8,128)(2,1)S(1)}, u32[]{:S(2)}, u32[]{:S(2)}) async-start(bf16[8,8,3584]{2,1,0:T(8,128)(2,1)} %fusion.1), calls=%async_computation | async-start | bytes 917504 | tf_op jit(solution)/shard_map/all_to_all | solution.py:86
  27.1 3.8 %collective-permute-start.5 = (bf16[1,8,3584]{2,1,0:T(8,128)(2,1)S(1)}, bf16[1,8,3584]{2,1,0:T(8,128)(2,1)S(1)}, u32[]{:S(2)}, u32[]{:S(2)}) collective-permute-start(bf16[1,8,3584]{2,1,0:T(8,128)(2,1)S(1)} %get-tuple-element.7), channel_id=1, source_target_pairs={{0,12},{2,14},{4,8},{6,10},{8,4},{10,6},{12,0},{14,2},{1,13},{3,15... | collective-permute-start | bytes 172040 | tf_op jit(solution)/shard_map/ppermute | solution.py:22
  31.0 1.5 collective-permute-start.6
  32.6 6.5 %collective-permute-done.5 = bf16[1,8,3584]{2,1,0:T(8,128)(2,1)S(1)} collective-permute-done((bf16[1,8,3584]{2,1,0:T(8,128)(2,1)S(1)}, bf16[1,8,3584]{2,1,0:T(8,128)(2,1)S(1)}, u32[]{:S(2)}, u32[]{:S(2)}) %collective-permute-start.5) | collective-permute-done | bytes 57376 | tf_op jit(solution)/shard_map/ppermute | solution.py:22
  39.1 1.6 collective-permute-done.6
  40.6 9.7 %fusion.11 = f32[64,2048]{1,0:T(8,128)S(1)} fusion(bf16[2048,3584]{1,0:T(8,128)(2,1)} %param.15, bf16[8,8,3584]{2,1,0:T(8,128)(2,1)S(1)} %constant_dynamic-update-slice_fusion.6), kind=kOutput, calls=%fused_computation.19 | convolution fusion | flops 939524096 | bytes 15663104 | tf_op jit(solution)/shard_map/nd,hd->nh/dot_general | solution.py:28
  50.3 9.7 %fusion.13 = f32[64,2048]{1,0:T(8,128)S(1)} fusion(bf16[2048,3584]{1,0:T(8,128)(2,1)} %param.16, bf16[8,8,3584]{2,1,0:T(8,128)(2,1)S(1)} %constant_dynamic-update-slice_fusion.6), kind=kOutput, calls=%fused_computation.21 | convolution fusion | flops 939524096 | bytes 15663104 | tf_op jit(solution)/shard_map/nd,hd->nh/dot_general | solution.py:29
  60.0 9.7 %multiply_convert_fusion.1 = (bf16[64,2048]{1,0:T(8,128)(2,1)S(1)}, bf16[64,2048]{1,0:T(8,128)(2,1)S(1)}) fusion(f32[64,2048]{1,0:T(8,128)S(1)} %fusion.11, f32[64,2048]{1,0:T(8,128)S(1)} %fusion.13, bf16[2048,3584]{1,0:T(8,128)(2,1)} %param.17, bf16[8,8,3584]{2,1,0:T(8,128)(2,1)S(1)} %all-to-all-done), kind=kOutput, calls=%fused_computation.11 | convolution fusion | flops 941228032 | bytes 16711680 | tf_op jit(solution)/shard_map/nd,hd->nh/dot_general | solution.py:33
  69.7 11.8 %fusion.7 = f32[2048,3584]{1,0:T(8,128)} fusion(bf16[64,2048]{1,0:T(8,128)(2,1)S(1)} %get-tuple-element.4, bf16[8,8,3584]{2,1,0:T(8,128)(2,1)S(1)} %constant_dynamic-update-slice_fusion.6), kind=kOutput, calls=%fused_computation.15 | convolution fusion | flops 939524096 | bytes 30081024 | tf_op jit(solution)/shard_map/nh,nd->hd/dot_general | solution.py:41
  81.5 0.2 reduce-scatter.8.cloned.1.call-start
  81.7 15.6 %fusion.15 = f32[2048,3584]{1,0:T(8,128)} fusion(bf16[8,8,3584]{2,1,0:T(8,128)(2,1)S(1)} %all-to-all-done, f32[64,2048]{1,0:T(8,128)S(1)} %fusion.13, f32[64,2048]{1,0:T(8,128)S(1)} %fusion.11), kind=kOutput, calls=%fused_computation.23 | convolution fusion | flops 940310528 | bytes 30867456 | tf_op jit(solution)/shard_map/nh,nd->hd/dot_general | solution.py:42
  97.4 18.9 %fusion.9 = f32[2048,3584]{1,0:T(8,128)} fusion(bf16[64,2048]{1,0:T(8,128)(2,1)S(1)} %get-tuple-element.5, bf16[8,8,3584]{2,1,0:T(8,128)(2,1)S(1)} %constant_dynamic-update-slice_fusion.6), kind=kOutput, calls=%fused_computation.17 | convolution fusion | flops 939524096 | bytes 30081024 | tf_op jit(solution)/shard_map/nh,nd->hd/dot_general | solution.py:38
  116.4 9.6 %fusion.27 = f32[64,3584]{1,0:T(8,128)S(1)} fusion(bf16[64,2048]{1,0:T(8,128)(2,1)S(1)} %get-tuple-element.5, bf16[2048,3584]{1,0:T(8,128)(2,1)} %param.15), kind=kOutput, calls=%fused_computation.59 | convolution fusion | flops 939524096 | bytes 15859712 | tf_op jit(solution)/shard_map/dot_general | solution.py:43
  126.0 7.8 %fusion.3 = bf16[8,8,3584]{2,1,0:T(8,128)(2,1)S(1)} fusion(f32[64,3584]{1,0:T(8,128)S(1)} %fusion.27, bf16[64,2048]{1,0:T(8,128)(2,1)S(1)} %get-tuple-element.4, bf16[2048,3584]{1,0:T(8,128)(2,1)} %param.16), kind=kOutput, calls=%fused_computation.7 | convolution fusion | flops 939982848 | bytes 16318464 | tf_op jit(solution)/shard_map/dot_general | solution.py:45
  133.8 17.9 %all_to_all.10 = bf16[8,8,3584]{2,1,0:T(8,128)(2,1)S(1)} all-to-all(bf16[8,8,3584]{2,1,0:T(8,128)(2,1)S(1)} %fusion.3), channel_id=1, replica_groups=mesh['groups'=2,'expert'=8,'dp'=2] {'expert'}, dimensions={0} | all-to-all | bytes 917504 | tf_op jit(solution)/shard_map/all_to_all | solution.py:95
  151.8 1.4 fusion
  153.1 12.6 %convert_element_type.44 = bf16[1024,3584]{1,0:T(8,128)(2,1)} convert(f32[1024,3584]{1,0:T(8,128)} %reduce-scatter.6.cloned.1.call-done) | non-fusion elementwise | flops 3670016 | bytes 22020096 | tf_op jit(solution)/shard_map/convert_element_type | solution.py:110
  165.7 1.3 reduce-scatter.8.cloned.1.call-done
  167.0 9.2 %convert_element_type.46 = bf16[1024,3584]{1,0:T(8,128)(2,1)} convert(f32[1024,3584]{1,0:T(8,128)} %reduce-scatter.8.cloned.1.call-done) | non-fusion elementwise | flops 3670016 | bytes 22020096 | tf_op jit(solution)/shard_map/convert_element_type | solution.py:111
  176.2 34.6 %reduce-scatter.4.cloned.1.call-done = f32[1024,3584]{1,0:T(8,128)} async-done(((f32[2048,3584]{1,0:T(8,128)}), f32[1024,3584]{1,0:T(8,128)}) %reduce-scatter.4.cloned.1.call-update) | async-done | bytes 14680080 | tf_op jit(solution)/shard_map/reduce_scatter | solution.py:103
  210.8 9.1 %convert_element_type.43 = bf16[1024,3584]{1,0:T(8,128)(2,1)} convert(f32[1024,3584]{1,0:T(8,128)} %reduce-scatter.4.cloned.1.call-done) | non-fusion elementwise | flops 3670016 | bytes 22020096 | tf_op jit(solution)/shard_map/convert_element_type | solution.py:109
  (36 shorter events, 0.7 us)
Async XLA Ops:
  7.2 2.7 %copy-start = (bf16[128,3584]{1,0:T(8,128)(2,1)S(1)}, bf16[128,3584]{1,0:T(8,128)(2,1)}, u32[]{:S(2)}) copy-start(bf16[128,3584]{1,0:T(8,128)(2,1)} %param.9) | copy-start | bytes 2752516
  10.2 16.9 %collective-permute-start = (bf16[1,8,3584]{2,1,0:T(8,128)(2,1)S(1)}, bf16[1,8,3584]{2,1,0:T(8,128)(2,1)S(1)}, u32[]{:S(2)}, u32[]{:S(2)}) collective-permute-start(bf16[1,8,3584]{2,1,0:T(8,128)(2,1)S(1)} %get-tuple-element.12), channel_id=1, source_target_pairs={{0,2},{2,0},{4,6},{6,4},{8,10},{10,8},{12,14},{14,12},{1,3},{3,1},... | collective-permute-start | bytes 172040 | tf_op jit(solution)/shard_map/ppermute | solution.py:22
  13.2 17.7 %collective-permute-start.1 = (bf16[1,8,3584]{2,1,0:T(8,128)(2,1)S(1)}, bf16[1,8,3584]{2,1,0:T(8,128)(2,1)S(1)}, u32[]{:S(2)}, u32[]{:S(2)}) collective-permute-start(bf16[1,8,3584]{2,1,0:T(8,128)(2,1)S(1)} %get-tuple-element.11), channel_id=1, source_target_pairs={{0,4},{2,6},{4,0},{6,2},{8,12},{10,14},{12,8},{14,10},{1,5},{3,7},... | collective-permute-start | bytes 172040 | tf_op jit(solution)/shard_map/ppermute | solution.py:22
  14.8 17.7 %collective-permute-start.2 = (bf16[1,8,3584]{2,1,0:T(8,128)(2,1)S(1)}, bf16[1,8,3584]{2,1,0:T(8,128)(2,1)S(1)}, u32[]{:S(2)}, u32[]{:S(2)}) collective-permute-start(bf16[1,8,3584]{2,1,0:T(8,128)(2,1)S(1)} %get-tuple-element.10), channel_id=1, source_target_pairs={{0,6},{2,4},{4,2},{6,0},{8,14},{10,12},{12,10},{14,8},{1,7},{3,5},... | collective-permute-start | bytes 172040 | tf_op jit(solution)/shard_map/ppermute | solution.py:22
  14.8 17.7 %collective-permute-start.3 = (bf16[1,8,3584]{2,1,0:T(8,128)(2,1)S(1)}, bf16[1,8,3584]{2,1,0:T(8,128)(2,1)S(1)}, u32[]{:S(2)}, u32[]{:S(2)}) collective-permute-start(bf16[1,8,3584]{2,1,0:T(8,128)(2,1)S(1)} %get-tuple-element.9), channel_id=1, source_target_pairs={{0,8},{2,10},{4,12},{6,14},{8,0},{10,2},{12,4},{14,6},{1,9},{3,11}... | collective-permute-start | bytes 172040 | tf_op jit(solution)/shard_map/ppermute | solution.py:22
  17.8 14.7 %collective-permute-start.4 = (bf16[1,8,3584]{2,1,0:T(8,128)(2,1)S(1)}, bf16[1,8,3584]{2,1,0:T(8,128)(2,1)S(1)}, u32[]{:S(2)}, u32[]{:S(2)}) collective-permute-start(bf16[1,8,3584]{2,1,0:T(8,128)(2,1)S(1)} %get-tuple-element.8), channel_id=1, source_target_pairs={{0,10},{2,8},{4,14},{6,12},{8,2},{10,0},{12,6},{14,4},{1,11},{3,9}... | collective-permute-start | bytes 172040 | tf_op jit(solution)/shard_map/ppermute | solution.py:22
  22.2 37.8 %all-to-all-start = ((bf16[8,8,3584]{2,1,0:T(8,128)(2,1)}), bf16[8,8,3584]{2,1,0:T(8,128)(2,1)S(1)}, u32[]{:S(2)}, u32[]{:S(2)}) async-start(bf16[8,8,3584]{2,1,0:T(8,128)(2,1)} %fusion.1), calls=%async_computation | async-start | bytes 917504 | tf_op jit(solution)/shard_map/all_to_all | solution.py:86
  27.1 126.1 %reduce-scatter.6.cloned.1.call-start = ((), (), s32[]{:S(2)}) async-start(), calls=%async_computation.6 | async-start | bytes 44040192 | tf_op jit(solution)/shard_map/reduce_scatter | solution.py:104
  27.1 12.0 %collective-permute-start.5 = (bf16[1,8,3584]{2,1,0:T(8,128)(2,1)S(1)}, bf16[1,8,3584]{2,1,0:T(8,128)(2,1)S(1)}, u32[]{:S(2)}, u32[]{:S(2)}) collective-permute-start(bf16[1,8,3584]{2,1,0:T(8,128)(2,1)S(1)} %get-tuple-element.7), channel_id=1, source_target_pairs={{0,12},{2,14},{4,8},{6,10},{8,4},{10,6},{12,0},{14,2},{1,13},{3,15... | collective-permute-start | bytes 172040 | tf_op jit(solution)/shard_map/ppermute | solution.py:22
  31.0 9.7 %collective-permute-start.6 = (bf16[1,8,3584]{2,1,0:T(8,128)(2,1)S(1)}, bf16[1,8,3584]{2,1,0:T(8,128)(2,1)S(1)}, u32[]{:S(2)}, u32[]{:S(2)}) collective-permute-start(bf16[1,8,3584]{2,1,0:T(8,128)(2,1)S(1)} %get-tuple-element.6), channel_id=1, source_target_pairs={{0,14},{2,12},{4,10},{6,8},{8,6},{10,4},{12,2},{14,0},{1,15},{3,13... | collective-permute-start | bytes 172040 | tf_op jit(solution)/shard_map/ppermute | solution.py:22
  81.5 85.5 %reduce-scatter.8.cloned.1.call-start = ((), (), s32[]{:S(2)}) async-start(), calls=%async_computation.7 | async-start | bytes 44040192 | tf_op jit(solution)/shard_map/reduce_scatter | solution.py:105
  97.4 113.4 %reduce-scatter.4.cloned.1.call-start = ((), (), s32[]{:S(2)}) async-start(), calls=%async_computation.5 | async-start | bytes 44040192 | tf_op jit(solution)/shard_map/reduce_scatter | solution.py:103
  167.0 52.8 %copy-start.1 = (bf16[128,3584]{1,0:T(8,128)(2,1)S(1)}, bf16[128,3584]{1,0:T(8,128)(2,1)}, u32[]{:S(2)}) copy-start(bf16[128,3584]{1,0:T(8,128)(2,1)} %param.9) | copy-start | bytes 2752516
Sparse Core Ops, SparseCore 0:
  81.6 41.4 reduce-scatter.5
  125.4 41.5 reduce-scatter.7
  169.3 41.3 reduce-scatter.3
